TPU v7x, 1024 devices: a whole 8x8x8 slice. The times are simulated.
1024 devices in a mesh: seq: 32 (over y_hi, z, core), dp: 32 (over x, y_lo).
Axes of the slice: x: 8, y: 8 (y_hi: 2, y_lo: 4; y = y_hi * 4 + y_lo), z: 8, core: 2. Of those that a mesh axis runs over, the one named last changes fastest.
Arguments:
- skip_input: bfloat16 [64, 8192, 768], P('dp', 'seq'), may hold values from -6 to 6
- upstream: bfloat16 [64, 8192, 1280], P('dp', 'seq'), may hold values from -6 to 6
- proj_weight: bfloat16 [768, 1280], replicated, may hold values from -0.21875 to 0.21875
- depth_kernel: float32 [3, 1280], replicated, may hold values from -3 to 3
Outputs:
- input_grad: bfloat16 [64, 8192, 768], P('dp', 'seq')
- weight_grad: float32 [768, 1280], P('dp', 'seq')
All inputs are finite; a program needn't handle non-finite values.
Results may differ from a plain program's by a relative error of at most 0.0053.
Values may be sent and summed in bfloat16 or wider, within the bound.
A program may use at most 32 MiB of HBM per device.

v0:
```python
import jax
import jax.numpy as jnp
from jax import lax
from jax.sharding import PartitionSpec as P


def padded_2(block, sides, width):
    for axis, dim in sides:
        count = lax.axis_size(axis)
        forward = [(i, i + 1) for i in range(count - 1)]
        backward = [(target, source) for source, target in forward]
        low = lax.ppermute(
            lax.slice_in_dim(block, block.shape[dim] - width, None, axis=dim), axis, forward
        )
        high = lax.ppermute(lax.slice_in_dim(block, 0, width, axis=dim), axis, backward)
        block = jnp.concatenate([low, block, high], axis=dim)
    return block


def gelu_slope(pre, scaled):
    return jax.vjp(jax.nn.gelu, pre)[1](scaled)[0]


def on_device(skip_input, upstream, proj_weight, depth_kernel):
    batch = skip_input.shape[0]
    k_left = depth_kernel[0]
    k_mid = depth_kernel[1]
    k_right = depth_kernel[2]
    proj = jnp.einsum(
        "bpc,cf->bpf", skip_input, proj_weight, preferred_element_type=jnp.float32
    ).astype(jnp.bfloat16)
    padded = padded_2(proj, (("seq", 1),), 1)
    proj_wide = padded.astype(jnp.float32)
    before = proj_wide[:, :-2]
    centre = proj_wide[:, 1:-1]
    after = proj_wide[:, 2:]
    halved = 0.5 * upstream.astype(jnp.float32)
    slope_fwd = gelu_slope(k_left * before + k_mid * centre + k_right * after, halved)
    slope_rev = gelu_slope(k_right * before + k_mid * centre + k_left * after, halved)
    slopes = padded_2(jnp.stack([slope_fwd, slope_rev]), (("seq", 2),), 1)
    fwd_wide = slopes[0]
    rev_wide = slopes[1]
    grad_proj = (
        k_left * (fwd_wide[:, 2:] + rev_wide[:, :-2])
        + k_mid * (fwd_wide[:, 1:-1] + rev_wide[:, 1:-1])
        + k_right * (fwd_wide[:, :-2] + rev_wide[:, 2:])
    ).astype(jnp.bfloat16)
    input_grad = jnp.einsum(
        "bpf,cf->bpc", grad_proj, proj_weight, preferred_element_type=jnp.float32
    ).astype(jnp.bfloat16)
    partial_value = lax.dot_general(
        skip_input, grad_proj, (((0, 1), (0, 1)), ((), ())), preferred_element_type=jnp.float32
    )
    samples = batch * lax.axis_size("dp")
    section_one = lax.psum_scatter(partial_value, "seq", scatter_dimension=1, tiled=True)
    reduced = lax.psum_scatter(section_one, "dp", scatter_dimension=0, tiled=True)
    return (input_grad, reduced / samples)


def solution(mesh):
    return jax.shard_map(
        on_device,
        mesh=mesh,
        in_specs=(P("dp", "seq", None), P("dp", "seq", None), P(), P()),
        out_specs=(P("dp", "seq", None), P("dp", "seq")),
        check_vma=False,
    )
```

profile of v0, /device:TPU:16, one launch (start us, length us, event | category | flops | bytes accessed | tf_op | source)
XLA Modules:
  0.0 508.3 jit_solution(15890073078365457728)
XLA Ops:
  7.2 0.0 copy-start
  7.2 0.0 copy-start.2
  7.2 0.0 reduce-scatter.3.cloned.1.call-start
  7.2 1.5 copy-done
  8.7 2.3 convolution_convert_fusion
  11.0 0.0 copy-start.1
  11.1 1.9 collective-permute-start
  13.0 1.3 collective-permute-start.1
  14.3 0.0 copy-done.2
  14.3 0.0 collective-permute-done
  14.3 4.8 collective-permute-done.1
  19.1 0.3 maximum_convert_fusion
  19.4 0.0 copy-done.1
  19.4 4.7 fusion.6
  24.2 4.3 collective-permute-start.2
  28.5 1.3 collective-permute-start.3
  29.8 0.0 collective-permute-done.2
  29.8 2.3 collective-permute-done.3
  32.1 0.5 pad_maximum_fusion
  32.6 0.3 slice_bitcast_fusion.1
  33.0 0.0 copy-start.3
  33.0 1.4 fusion.16
  34.4 3.1 convolution_bitcast_fusion
  37.5 0.0 reduce-scatter.3.cloned.1.call-update
  37.5 0.0 all-reduce.3.cloned.1.call-start
  37.6 1.3 dynamic-slice
  39.5 174.6 %reduce-scatter.3.cloned.1.call-done = f32[768,40]{0,1:T(8,128)} async-done(((f32[768,1280]{0,1:T(8,128)}), f32[768,40]{0,1:T(8,128)}) %reduce-scatter.3.cloned.1.call-update) | async-done | bytes 122896 | tf_op jit(solution)/shard_map/reduce_scatter | solution.py:55
  214.1 0.0 all-reduce.3.cloned.1.call-update
  214.1 2.1 fusion.23
  216.2 283.7 %all-reduce.3.cloned.1.call-done = f32[768,40]{0,1:T(8,128)} async-done(((f32[768,40]{0,1:T(8,128)}), f32[768,40]{0,1:T(8,128)}) %all-reduce.3.cloned.1.call-update) | async-done | bytes 122896
  499.9 0.9 dynamic-slice_multiply_fusion
  500.8 0.7 copy.9
  (4 shorter events, 0.1 us)
Async XLA Ops:
  7.2 1.6 copy-start
  7.2 7.1 %copy-start.2 = (f32[3,1280]{1,0:T(4,128)S(1)}, f32[3,1280]{1,0:T(4,128)}, u32[]{:S(2)}) copy-start(f32[3,1280]{1,0:T(4,128)} %param.7) | copy-start | bytes 46084
  7.2 206.9 %reduce-scatter.3.cloned.1.call-start = ((), (), s32[]{:S(2)}) async-start(), calls=%async_computation.1 | async-start | bytes 4055040 | tf_op jit(solution)/shard_map/reduce_scatter | solution.py:55
  11.0 8.3 %copy-start.1 = (bf16[2,256,1280]{2,1,0:T(8,128)(2,1)S(1)}, bf16[2,256,1280]{2,1,0:T(8,128)(2,1)}, u32[]{:S(2)}) copy-start(bf16[2,256,1280]{2,1,0:T(8,128)(2,1)} %param.5) | copy-start | bytes 3932164
  11.1 3.2 collective-permute-start
  13.0 6.1 %collective-permute-start.1 = (bf16[2,1,1280]{2,1,0:T(2,128)(2,1)S(1)}, bf16[2,1,1280]{2,1,0:T(2,128)(2,1)S(1)}, u32[]{:S(2)}, u32[]{:S(2)}) collective-permute-start(bf16[2,1,1280]{2,1,0:T(2,128)(2,1)S(1)} %get-tuple-element.16), channel_id=1, source_target_pairs={{32,0},{64,32},{96,64},{128,96},{160,128},{192,160},{224,192},{256... | collective-permute-start | bytes 15368 | tf_op jit(solution)/shard_map/ppermute | solution.py:15
  24.2 5.6 %collective-permute-start.2 = (f32[2,2,1,1280]{3,2,1,0:T(1,128)S(1)}, f32[2,2,1,1280]{3,2,1,0:T(1,128)S(1)}, u32[]{:S(2)}, u32[]{:S(2)}) collective-permute-start(f32[2,2,1,1280]{3,2,1,0:T(1,128)S(1)} %get-tuple-element.11), channel_id=1, source_target_pairs={{0,32},{32,64},{64,96},{96,128},{128,160},{160,192},{192,224},{224... | collective-permute-start | bytes 61448 | tf_op jit(solution)/shard_map/ppermute | solution.py:12
  28.5 3.6 collective-permute-start.3
  33.0 1.4 copy-start.3
  37.5 462.4 %all-reduce.3.cloned.1.call-start = ((), (), s32[]{:S(2)}) async-start(), calls=%async_computation.2 | async-start | bytes 245760
Sparse Core Ops, SparseCore 0:
  37.6 176.4 reduce-scatter.2
  217.6 282.2 all-reduce.2
where the time goes:
time: 509 us; the launch traced here: 508 us
  waiting for transfers between devices  465 us (91%)
  between operations  14.9 us (3%)
  starting transfers between devices  8.86 us (2%)
  other arithmetic  7.85 us (2%)
  matrix products  7.49 us (1%)
    unnamed x3, waiting for transfers between devices  284 us
    reduce_scatter x1, waiting for transfers between devices, on_device(): lax.psum_scatter(partial_value, 'seq', scatter_dimension=1, tiled=True)  175 us
  transfers between devices with their start and end apart: 6, of which 4 were waited for; matrix products, arithmetic and copies ran while one was open for 1% of the time, Pallas kernels for 0%

commit v1 on v0

v1 whole, which is shorter than its diff:
```python
import functools
import math

import jax
import jax.numpy as jnp
from jax import lax
from jax.experimental import pallas as pl
from jax.experimental.pallas import tpu as pltpu
from jax.sharding import PartitionSpec as P

MESH = pl.DeviceIdType.MESH
F32 = jnp.float32
BF16 = jnp.bfloat16
LANES = 128
EDGE = 16
Z, Y_LO, X, Y = 8, 4, 8, 8
STEPS = 5
C0 = math.sqrt(2.0 / math.pi)
C1 = 0.044715 * C0


def aligned(value, by):
    return pl.multiple_of(value, by)


def kernel(
    skip_hbm, up_hbm, w_hbm, taps_ref, ig_hbm, wg_ref,
    skipx, upx, w_v, skip_t, projx, a_buf, b_buf, m_buf, gp_v, gp_c, own, core_out, core_in,
    s1, r1x, r1y, s2, r2, s3, r3, ig_v,
    in_sem, halo_send, halo_recv, core_send, core_recv, s1_send, r1x_recv, r1y_recv,
    s2_send, r2_recv, s3_send, r3_recv, out_sem,
):
    seq, dp = lax.axis_index("seq"), lax.axis_index("dp")
    n_seq = 4 * Z
    core = lax.rem(seq, 2)
    z = lax.rem(lax.div(seq, 2), Z)
    y_hi = lax.div(seq, 2 * Z)
    x, y_lo = lax.div(dp, Y_LO), lax.rem(dp, Y_LO)
    y = y_hi * Y_LO + y_lo
    batch, length, channels = skip_hbm.shape
    wide = up_hbm.shape[2]
    half = wide // 2
    rows = batch * length
    ext = length + 2 * EDGE

    def device(xx, yy, zz, cc):
        return {
            "seq": lax.div(yy, Y_LO) * (2 * Z) + zz * 2 + cc,
            "dp": xx * Y_LO + lax.rem(yy, Y_LO),
        }

    loads = [
        pltpu.make_async_copy(skip_hbm, skipx.at[:, pl.ds(EDGE, length)], in_sem.at[0]),
        pltpu.make_async_copy(w_hbm, w_v, in_sem.at[1]),
        pltpu.make_async_copy(up_hbm, upx.at[:, pl.ds(EDGE, length)], in_sem.at[2]),
    ]
    for load in loads:
        load.start()

    barrier = pltpu.get_barrier_semaphore()

    def greet(target):
        pl.semaphore_signal(barrier, inc=1, device_id=target, device_id_type=MESH)

    @pl.when(seq > 0)
    def _():
        greet({"seq": seq - 1, "dp": dp})

    @pl.when(seq < n_seq - 1)
    def _():
        greet({"seq": seq + 1, "dp": dp})

    @pl.loop(1, 8)
    def _(e):
        greet(device(lax.rem(x + e, X), y, z, core))
        greet(device(x, lax.rem(y + e, Y), z, core))

    @pl.loop(1, 16)
    def _(e):
        greet(device(x, y, lax.rem(z + lax.div(e, 2), Z), lax.rem(core + e, 2)))

    has_left = jnp.where(seq > 0, 1, 0)
    has_right = jnp.where(seq < n_seq - 1, 1, 0)
    pl.semaphore_wait(barrier, 29 + has_left + has_right)

    low, high = pl.ds(0, EDGE), pl.ds(length + EDGE, EDGE)

    def halo(k, source, target, side, place, to):
        return pltpu.make_async_remote_copy(
            src_ref=source.at[:, side], dst_ref=target.at[:, place],
            send_sem=halo_send.at[k], recv_sem=halo_recv.at[k],
            device_id={"seq": to, "dp": dp}, device_id_type=MESH,
        )

    first, last = pl.ds(0, EDGE), pl.ds(length - EDGE, EDGE)

    def to_right():
        return [halo(0, skip_hbm, skipx, last, low, seq + 1), halo(1, up_hbm, upx, last, low, seq + 1)]

    def to_left():
        return [halo(2, skip_hbm, skipx, first, high, seq - 1), halo(3, up_hbm, upx, first, high, seq - 1)]

    @pl.when(seq < n_seq - 1)
    def _():
        for copy in to_right():
            copy.start()

    @pl.when(seq > 0)
    def _():
        for copy in to_left():
            copy.start()

    @pl.when(seq == 0)
    def _():
        skipx[:, low] = jnp.zeros((batch, EDGE, channels), BF16)
        upx[:, low] = jnp.zeros((batch, EDGE, wide), BF16)

    @pl.when(seq == n_seq - 1)
    def _():
        skipx[:, high] = jnp.zeros((batch, EDGE, channels), BF16)
        upx[:, high] = jnp.zeros((batch, EDGE, wide), BF16)

    s2[...] = jnp.zeros_like(s2)

    loads[0].wait()
    for b in range(batch):
        skip_t[:, b * length : (b + 1) * length] = skipx[b, EDGE : EDGE + length].T
    loads[1].wait()

    def rounded(lhs, columns):
        return jnp.dot(lhs, w_v[:, columns], preferred_element_type=F32).astype(BF16).astype(F32)

    @pl.loop(0, STEPS)
    def _(n):
        columns = pl.ds(aligned(n * 256, 256), 256)
        for b in range(batch):
            projx[b, 8 + EDGE : 8 + EDGE + length, columns] = rounded(skipx[b, EDGE : EDGE + length], columns)

    loads[2].wait()

    @pl.when(seq > 0)
    def _():
        for copy in to_right():
            copy.wait_recv()

    @pl.when(seq < n_seq - 1)
    def _():
        for copy in to_left():
            copy.wait_recv()

    @pl.loop(0, STEPS)
    def _(n):
        columns = pl.ds(aligned(n * 256, 256), 256)
        edges = jnp.concatenate(
            [skipx[b, side] for b in range(batch) for side in (low, high)], axis=0
        )
        edges = rounded(edges, columns)
        for b in range(batch):
            projx[b, 8 : 8 + EDGE, columns] = edges[2 * b * EDGE : (2 * b + 1) * EDGE]
            projx[b, 8 + EDGE + length : 8 + ext, columns] = edges[(2 * b + 1) * EDGE : (2 * b + 2) * EDGE]

    block = 32

    def slope(pre, quarter):
        square = pre * pre
        t = jnp.tanh(pre * (C0 + C1 * square))
        return quarter * (1.0 + t) * (1.0 + (pre - pre * t) * (C0 + (3.0 * C1) * square))

    def grads(b, offset, place):
        columns = pl.ds(offset, LANES)
        k_left, k_mid, k_right = (taps_ref[i : i + 1, columns] for i in range(3))
        k_sum, k_dif = 0.5 * (k_left + k_right), 0.5 * (k_left - k_right)

        @pl.loop(0, ext // block)
        def _(i):
            base = aligned(i * block, block)
            near = projx[b, pl.ds(base, block + 16), columns]
            before, centre, after = near[7 : 7 + block], near[8 : 8 + block], near[9 : 9 + block]
            even = k_mid * centre + k_sum * (before + after)
            odd = k_dif * (before - after)
            quarter = 0.25 * upx[b, pl.ds(base, block), columns].astype(F32)
            fwd, rev = slope(even + odd, quarter), slope(even - odd, quarter)
            both = fwd + rev
            even, odd = k_sum * both, k_dif * (fwd - rev)
            here = pl.ds(base, block)
            a_buf[here], b_buf[here], m_buf[here] = even + odd, even - odd, k_mid * both

        @pl.loop(0, length // block)
        def _(i):
            base = aligned(i * block, block)
            ahead = a_buf[pl.ds(base + 16, block + 8)][1 : 1 + block]
            behind = b_buf[pl.ds(base + 8, block + 8)][7 : 7 + block]
            value = (ahead + behind + m_buf[pl.ds(base + EDGE, block)]).astype(BF16)
            out = pl.ds(aligned(b * length + base, block), block)
            gp_v[out, columns] = value
            gp_c[out, place] = value

    def core_copy(j):
        return pltpu.make_async_remote_copy(
            src_ref=core_out.at[j], dst_ref=core_in.at[j],
            send_sem=core_send.at[j], recv_sem=core_recv.at[j],
            device_id=device(x, y, z, 1 - core), device_id_type=MESH,
        )

    def along_x(j, e):
        to = lax.rem(x + e, X)
        return pltpu.make_async_remote_copy(
            src_ref=s1.at[j, to], dst_ref=r1x.at[j, e],
            send_sem=s1_send.at[j], recv_sem=r1x_recv.at[j],
            device_id=device(to, y, z, core), device_id_type=MESH,
        )

    def along_y(j, e):
        to = lax.rem(y + e, Y)
        return pltpu.make_async_remote_copy(
            src_ref=s1.at[j, :, lax.rem(to, Y_LO)], dst_ref=r1y.at[lax.div(j, 2), e],
            send_sem=s1_send.at[j], recv_sem=r1y_recv.at[lax.div(j, 2)],
            device_id=device(x, to, z, core), device_id_type=MESH,
        )

    def scatter(j):
        core_copy(j).wait_recv()

        @pl.loop(0, X)
        def _(i):
            part = pl.ds(aligned(i * 96, 96), 96)
            total = own[j, part] + core_in[j, part]
            s1[j, i] = total.reshape(Y_LO, 3, 8, LANES).astype(BF16)

        @pl.when(core == 0)
        def _():
            @pl.loop(1, 8)
            def _(e):
                along_x(j, e).start()

        @pl.when(core == 1)
        def _():
            @pl.loop(1, 8)
            def _(e):
                @pl.when(lax.div(lax.rem(y + e, Y), Y_LO) == lax.rem(j + 1, 2))
                def _():
                    along_y(j, e).start()

    @pl.loop(0, STEPS)
    def _(j):
        kept = lax.rem(j + core, 2)
        for b in range(batch):
            grads(b, aligned(kept * half + j * LANES, LANES), slice(0, LANES))
            grads(b, aligned((1 - kept) * half + j * LANES, LANES), slice(LANES, 2 * LANES))

        @pl.loop(0, 3)
        def _(i):
            part = pl.ds(aligned(i * 256, 256), 256)
            chunk = jnp.dot(skip_t[part], gp_c[...], preferred_element_type=F32)
            own[j, part] = chunk[:, :LANES]
            core_out[j, part] = chunk[:, LANES:]

        core_copy(j).start()

        @pl.when(j > 0)
        def _():
            scatter(j - 1)

    scatter(STEPS - 1)

    @pl.loop(0, rows // 128)
    def _(i):
        part = pl.ds(aligned(i * 128, 128), 128)
        ig_v[part] = lax.dot_general(
            gp_v[part], w_v[...], (((1,), (1,)), ((), ())), preferred_element_type=F32
        ).astype(BF16)

    stores = [
        pltpu.make_async_copy(ig_v.at[pl.ds(b * length, length)], ig_hbm.at[b], out_sem.at[b])
        for b in range(batch)
    ]
    for store in stores:
        store.start()

    @pl.when(core == 0)
    def _():
        @pl.loop(0, STEPS)
        def _(j):
            pltpu.make_async_copy(r1x.at[j, 1:8], r1x.at[j, 1:8], r1x_recv.at[j]).wait()
            total = s1[j, x].astype(F32)
            for e in range(1, 8):
                total = total + r1x[j, e].astype(F32)
            s2[pl.ds(lax.rem(j, 2) * Y_LO, Y_LO), lax.div(j, 2)] = total.astype(BF16)

    @pl.when(core == 1)
    def _():
        @pl.loop(0, 2 + y_hi)
        def _(i):
            pltpu.make_async_copy(r1y.at[i, 1:8], r1y.at[i, 1:8], r1y_recv.at[i]).wait()
            for part in range(X):
                total = s1[2 * i + 1 - y_hi, part, y_lo].astype(F32)
                for e in range(1, 8):
                    total = total + r1y[i, e, part].astype(F32)
                s2[part, i] = total.astype(BF16)

    place = jnp.where(core == 0, y, x)

    def second(e):
        to = lax.rem(place + e, 8)
        target = device(jnp.where(core == 0, x, to), jnp.where(core == 0, to, y), z, core)
        return pltpu.make_async_remote_copy(
            src_ref=s2.at[to], dst_ref=r2.at[e], send_sem=s2_send, recv_sem=r2_recv,
            device_id=target, device_id_type=MESH,
        )

    @pl.loop(1, 8)
    def _(e):
        second(e).start()

    pltpu.make_async_copy(r2.at[1:8], r2.at[1:8], r2_recv).wait()
    for i in range(3):
        total = s2[place, i].astype(F32)
        for e in range(1, 8):
            total = total + r2[e, i].astype(F32)
        s3[i] = total

    def slot(zz):
        return jnp.where(core == y_hi, lax.div(zz, 3), lax.div(zz, 4))

    @pl.loop(1, 16)
    def _(e):
        to = lax.rem(z + lax.div(e, 2), Z)
        pltpu.make_async_remote_copy(
            src_ref=s3.at[slot(to)], dst_ref=r3.at[e], send_sem=s3_send, recv_sem=r3_recv,
            device_id=device(x, y, to, lax.rem(core + e, 2)), device_id_type=MESH,
        ).start()

    pltpu.make_async_copy(r3.at[1:16], r3.at[1:16], r3_recv).wait()
    mine, other = s3[slot(z)], r3[1]
    for e in range(1, 8):
        mine = mine + r3[2 * e]
        other = other + r3[2 * e + 1]
    start = z * 80 + core * 40
    tile, offset = lax.div(start, LANES), lax.rem(start, LANES)
    mine_first = lax.rem(tile + core + y_hi, 2) == 0
    mine, other = mine.reshape(24, LANES), other.reshape(24, LANES)
    lead = jnp.where(mine_first, mine, other)
    trail = jnp.where(mine_first, other, mine)
    lane = lax.broadcasted_iota(jnp.int32, (24, LANES), 1)
    joined = jnp.where(lane >= offset, lead, trail)
    turned = pltpu.roll(joined, lax.rem(LANES - offset, LANES), 1)
    wg_ref[...] = turned[:, :40] * (1.0 / (batch * X * Y_LO))

    @pl.when(seq < n_seq - 1)
    def _():
        for copy in to_right():
            copy.wait_send()

    @pl.when(seq > 0)
    def _():
        for copy in to_left():
            copy.wait_send()

    @pl.loop(0, STEPS)
    def _(j):
        core_copy(j).wait_send()

        @pl.when(core == 0)
        def _():
            pltpu.make_async_copy(s1.at[j, 0:7], s1.at[j, 0:7], s1_send.at[j]).wait()

        @pl.when((core == 1) & (lax.rem(j + 1, 2) == y_hi))
        def _():
            pltpu.make_async_copy(r1y.at[0, 0:3], r1y.at[0, 0:3], s1_send.at[j]).wait()

        @pl.when((core == 1) & (lax.rem(j + 1, 2) != y_hi))
        def _():
            pltpu.make_async_copy(r1y.at[0, 0:4], r1y.at[0, 0:4], s1_send.at[j]).wait()

    pltpu.make_async_copy(s2.at[0:7], s2.at[0:7], s2_send).wait()
    pltpu.make_async_copy(r3.at[0:15], r3.at[0:15], s3_send).wait()
    for store in stores:
        store.wait()


def on_device(skip_input, upstream, proj_weight, depth_kernel):
    batch, length, channels = skip_input.shape
    wide = upstream.shape[2]
    ext = length + 2 * EDGE
    rows = batch * length
    vmem = pltpu.VMEM
    dma = pltpu.SemaphoreType.DMA
    return pl.pallas_call(
        kernel,
        out_shape=(
            jax.ShapeDtypeStruct((batch, length, channels), BF16),
            jax.ShapeDtypeStruct((24, 40), F32),
        ),
        in_specs=[
            pl.BlockSpec(memory_space=pl.ANY),
            pl.BlockSpec(memory_space=pl.ANY),
            pl.BlockSpec(memory_space=pl.ANY),
            pl.BlockSpec(memory_space=vmem),
        ],
        out_specs=(pl.BlockSpec(memory_space=pl.ANY), pl.BlockSpec(memory_space=vmem)),
        scratch_shapes=[
            vmem((batch, ext, channels), BF16),
            vmem((batch, ext, wide), BF16),
            vmem((channels, wide), BF16),
            vmem((channels, rows), BF16),
            vmem((batch, ext + 16, wide), F32),
            vmem((ext, LANES), F32),
            vmem((ext, LANES), F32),
            vmem((ext, LANES), F32),
            vmem((rows, wide), BF16),
            vmem((rows, 2 * LANES), BF16),
            vmem((STEPS, channels, LANES), F32),
            vmem((STEPS, channels, LANES), F32),
            vmem((STEPS, channels, LANES), F32),
            vmem((STEPS, X, Y_LO, 3, 8, LANES), BF16),
            vmem((STEPS, X, Y_LO, 3, 8, LANES), BF16),
            vmem((3, Y, X, 3, 8, LANES), BF16),
            vmem((8, 3, 3, 8, LANES), BF16),
            vmem((8, 3, 3, 8, LANES), BF16),
            vmem((3, 3, 8, LANES), F32),
            vmem((16, 3, 8, LANES), F32),
            vmem((rows, channels), BF16),
            dma((3,)), dma((4,)), dma((4,)), dma((STEPS,)), dma((STEPS,)),
            dma((STEPS,)), dma((STEPS,)), dma((3,)),
            dma, dma, dma, dma, dma((2,)),
        ],
        compiler_params=pltpu.CompilerParams(
            collective_id=0, has_side_effects=True, vmem_limit_bytes=56 * 1024 * 1024
        ),
        cost_estimate=pl.CostEstimate(flops=3 * 10**9, bytes_accessed=5 * 10**6, transcendentals=0),
    )(skip_input, upstream, proj_weight, depth_kernel)


def solution(mesh):
    return jax.shard_map(
        on_device,
        mesh=mesh,
        in_specs=(P("dp", "seq", None), P("dp", "seq", None), P(), P()),
        out_specs=(P("dp", "seq", None), P("dp", "seq")),
        check_vma=False,
    )
```

time: 509 us -> 71.2 us (0.14)
  the two profiles are of different devices: /device:TPU:16 before, /device:TPU:1 now
where the time goes in v1:
time: 71.2 us; the launch traced here: 70.9 us
  Pallas kernels  66.9 us (94%)
  local copies, waits for them, and re-layouts  3.37 us (5%)
    pallas_call x1, Pallas kernels, on_device(): pl.pallas_call(kernel, out_shape=(jax.ShapeDtypeStruct((batch, length, ch...  66.9 us
    unnamed x2, local copies, waits for them, and re-layouts  3.37 us

profile of v1, /device:TPU:1, one launch (start us, length us, event | category | flops | bytes accessed | tf_op | source)
XLA Modules:
  0.0 70.9 jit_solution(12102398490290117857)
XLA Ops:
  0.6 66.9 %shard_map.59 = (bf16[2,256,768]{2,1,0:T(8,128)(2,1)}, f32[24,40]{1,0:T(8,128)}) custom-call(bf16[2,256,768]{2,1,0:T(8,128)(2,1)} %skip_hbm.1, bf16[2,256,1280]{2,1,0:T(8,128)(2,1)} %up_hbm.1, bf16[768,1280]{1,0:T(8,128)(2,1)} %w_hbm.1, f32[3,1280]{1,0:T(4,128)} %taps_ref.1), custom_call_target="tpu_custom_call" | custom-call | flops 3000000000 | bytes 5000000 | tf_op jit(solution)/shard_map/pallas_call | solution.py:388
  67.5 2.1 %copy.8 = bf16[2,256,768]{2,1,0:T(8,128)(2,1)} copy(bf16[2,256,768]{2,1,0:T(8,128)(2,1)} %get-tuple-element.4) | data formatting | bytes 1572864
  69.6 1.3 %copy.9 = f32[24,40]{1,0:T(8,128)} copy(f32[24,40]{1,0:T(8,128)} %get-tuple-element.5) | data formatting | bytes 7680

commit v2 on v1

--- a/solution.py
+++ b/solution.py
@@ -13,6 +13,7 @@
 BF16 = jnp.bfloat16
 LANES = 128
 EDGE = 16
+BLOCK, BLOCK2 = 48, 64
 Z, Y_LO, X, Y = 8, 4, 8, 8
 STEPS = 5
 C0 = math.sqrt(2.0 / math.pi)
@@ -24,11 +25,11 @@
 
 
 def kernel(
-    skip_hbm, up_hbm, w_hbm, taps_ref, ig_hbm, wg_ref,
-    skipx, upx, w_v, skip_t, projx, a_buf, b_buf, m_buf, gp_v, gp_c, own, core_out, core_in,
-    s1, r1x, r1y, s2, r2, s3, r3, ig_v,
-    in_sem, halo_send, halo_recv, core_send, core_recv, s1_send, r1x_recv, r1y_recv,
-    s2_send, r2_recv, s3_send, r3_recv, out_sem,
+    skip_hbm, up_hbm, w_hbm, taps_ref, ig_ref, wg_ref,
+    skipx, upx, edge_up, w_v, skip_t, projx, a_buf, b_buf, m_buf, gp_v, own, core_out, core_in,
+    s1, r1x, r1y, s2, r2, s3, r3,
+    in_sem, w_sem, up_sem, halo_send, halo_recv, core_send, core_recv, s1_send, r1x_recv, r1y_recv,
+    s2_send, r2_recv, s3_send, r3_recv,
 ):
     seq, dp = lax.axis_index("seq"), lax.axis_index("dp")
     n_seq = 4 * Z
@@ -49,13 +50,28 @@
             "dp": xx * Y_LO + lax.rem(yy, Y_LO),
         }
 
-    loads = [
-        pltpu.make_async_copy(skip_hbm, skipx.at[:, pl.ds(EDGE, length)], in_sem.at[0]),
-        pltpu.make_async_copy(w_hbm, w_v, in_sem.at[1]),
-        pltpu.make_async_copy(up_hbm, upx.at[:, pl.ds(EDGE, length)], in_sem.at[2]),
-    ]
-    for load in loads:
-        load.start()
+    def natural(j, h):
+        return pl.ds(aligned(lax.rem(j + core + h, 2) * half + j * LANES, LANES), LANES)
+
+    def local(j, h):
+        return pl.ds(aligned((2 * j + h) * LANES, LANES), LANES)
+
+    load_skip = pltpu.make_async_copy(skip_hbm, skipx.at[:, pl.ds(EDGE, length)], in_sem)
+
+    def load_w(j, h):
+        return pltpu.make_async_copy(w_hbm.at[:, natural(j, h)], w_v.at[:, local(j, h)], w_sem.at[j, h])
+
+    def load_up(j, h):
+        target = upx.at[:, pl.ds(EDGE, length), local(j, h)]
+        return pltpu.make_async_copy(up_hbm.at[:, :, natural(j, h)], target, up_sem.at[j, h])
+
+    load_skip.start()
+
+    @pl.loop(0, STEPS)
+    def _(j):
+        for h in range(2):
+            load_w(j, h).start()
+            load_up(j, h).start()
 
     barrier = pltpu.get_barrier_semaphore()
 
@@ -95,10 +111,10 @@
     first, last = pl.ds(0, EDGE), pl.ds(length - EDGE, EDGE)
 
     def to_right():
-        return [halo(0, skip_hbm, skipx, last, low, seq + 1), halo(1, up_hbm, upx, last, low, seq + 1)]
+        return [halo(0, skip_hbm, skipx, last, low, seq + 1), halo(1, up_hbm, edge_up, last, pl.ds(0, EDGE), seq + 1)]
 
     def to_left():
-        return [halo(2, skip_hbm, skipx, first, high, seq - 1), halo(3, up_hbm, upx, first, high, seq - 1)]
+        return [halo(2, skip_hbm, skipx, first, high, seq - 1), halo(3, up_hbm, edge_up, first, pl.ds(EDGE, EDGE), seq - 1)]
 
     @pl.when(seq < n_seq - 1)
     def _():
@@ -113,30 +129,18 @@
     @pl.when(seq == 0)
     def _():
         skipx[:, low] = jnp.zeros((batch, EDGE, channels), BF16)
-        upx[:, low] = jnp.zeros((batch, EDGE, wide), BF16)
+        edge_up[:, 0:EDGE] = jnp.zeros((batch, EDGE, wide), BF16)
 
     @pl.when(seq == n_seq - 1)
     def _():
         skipx[:, high] = jnp.zeros((batch, EDGE, channels), BF16)
-        upx[:, high] = jnp.zeros((batch, EDGE, wide), BF16)
+        edge_up[:, EDGE : 2 * EDGE] = jnp.zeros((batch, EDGE, wide), BF16)
 
     s2[...] = jnp.zeros_like(s2)
 
-    loads[0].wait()
+    load_skip.wait()
     for b in range(batch):
         skip_t[:, b * length : (b + 1) * length] = skipx[b, EDGE : EDGE + length].T
-    loads[1].wait()
-
-    def rounded(lhs, columns):
-        return jnp.dot(lhs, w_v[:, columns], preferred_element_type=F32).astype(BF16).astype(F32)
-
-    @pl.loop(0, STEPS)
-    def _(n):
-        columns = pl.ds(aligned(n * 256, 256), 256)
-        for b in range(batch):
-            projx[b, 8 + EDGE : 8 + EDGE + length, columns] = rounded(skipx[b, EDGE : EDGE + length], columns)
-
-    loads[2].wait()
 
     @pl.when(seq > 0)
     def _():
@@ -149,51 +153,39 @@
             copy.wait_recv()
 
     @pl.loop(0, STEPS)
-    def _(n):
-        columns = pl.ds(aligned(n * 256, 256), 256)
-        edges = jnp.concatenate(
-            [skipx[b, side] for b in range(batch) for side in (low, high)], axis=0
-        )
-        edges = rounded(edges, columns)
-        for b in range(batch):
-            projx[b, 8 : 8 + EDGE, columns] = edges[2 * b * EDGE : (2 * b + 1) * EDGE]
-            projx[b, 8 + EDGE + length : 8 + ext, columns] = edges[(2 * b + 1) * EDGE : (2 * b + 2) * EDGE]
-
-    block = 32
+    def _(j):
+        for h in range(2):
+            for b in range(batch):
+                upx[b, low, local(j, h)] = edge_up[b, 0:EDGE, natural(j, h)]
+                upx[b, high, local(j, h)] = edge_up[b, EDGE : 2 * EDGE, natural(j, h)]
 
     def slope(pre, quarter):
         square = pre * pre
         t = jnp.tanh(pre * (C0 + C1 * square))
         return quarter * (1.0 + t) * (1.0 + (pre - pre * t) * (C0 + (3.0 * C1) * square))
 
-    def grads(b, offset, place):
-        columns = pl.ds(offset, LANES)
-        k_left, k_mid, k_right = (taps_ref[i : i + 1, columns] for i in range(3))
+    def grads(j, b, h):
+        here = slice(h * LANES, (h + 1) * LANES)
+        k_left, k_mid, k_right = (taps_ref[i : i + 1, natural(j, h)] for i in range(3))
         k_sum, k_dif = 0.5 * (k_left + k_right), 0.5 * (k_left - k_right)
-
-        @pl.loop(0, ext // block)
-        def _(i):
-            base = aligned(i * block, block)
-            near = projx[b, pl.ds(base, block + 16), columns]
-            before, centre, after = near[7 : 7 + block], near[8 : 8 + block], near[9 : 9 + block]
+        for base in range(0, ext, BLOCK):
+            near = projx[b, base : base + BLOCK + 16, here]
+            before, centre, after = near[7 : 7 + BLOCK], near[8 : 8 + BLOCK], near[9 : 9 + BLOCK]
             even = k_mid * centre + k_sum * (before + after)
             odd = k_dif * (before - after)
-            quarter = 0.25 * upx[b, pl.ds(base, block), columns].astype(F32)
+            quarter = 0.25 * upx[b, base : base + BLOCK, local(j, h)].astype(F32)
             fwd, rev = slope(even + odd, quarter), slope(even - odd, quarter)
             both = fwd + rev
             even, odd = k_sum * both, k_dif * (fwd - rev)
-            here = pl.ds(base, block)
-            a_buf[here], b_buf[here], m_buf[here] = even + odd, even - odd, k_mid * both
-
-        @pl.loop(0, length // block)
-        def _(i):
-            base = aligned(i * block, block)
-            ahead = a_buf[pl.ds(base + 16, block + 8)][1 : 1 + block]
-            behind = b_buf[pl.ds(base + 8, block + 8)][7 : 7 + block]
-            value = (ahead + behind + m_buf[pl.ds(base + EDGE, block)]).astype(BF16)
-            out = pl.ds(aligned(b * length + base, block), block)
-            gp_v[out, columns] = value
-            gp_c[out, place] = value
+            part = slice(base, base + BLOCK)
+            a_buf[b, part, here] = even + odd
+            b_buf[b, part, here] = even - odd
+            m_buf[b, part, here] = k_mid * both
+        for base in range(0, length, BLOCK2):
+            ahead = a_buf[b, base + 16 : base + 24 + BLOCK2, here][1 : 1 + BLOCK2]
+            behind = b_buf[b, base + 8 : base + 16 + BLOCK2, here][7 : 7 + BLOCK2]
+            value = (ahead + behind + m_buf[b, base + EDGE : base + EDGE + BLOCK2, here]).astype(BF16)
+            gp_v[b * length + base : b * length + base + BLOCK2, local(j, h)] = value
 
     def core_copy(j):
         return pltpu.make_async_remote_copy(
@@ -243,18 +235,21 @@
 
     @pl.loop(0, STEPS)
     def _(j):
-        kept = lax.rem(j + core, 2)
+        columns = pl.ds(aligned(j * 256, 256), 256)
+        for h in range(2):
+            load_w(j, h).wait()
+            load_up(j, h).wait()
         for b in range(batch):
-            grads(b, aligned(kept * half + j * LANES, LANES), slice(0, LANES))
-            grads(b, aligned((1 - kept) * half + j * LANES, LANES), slice(LANES, 2 * LANES))
-
-        @pl.loop(0, 3)
-        def _(i):
-            part = pl.ds(aligned(i * 256, 256), 256)
-            chunk = jnp.dot(skip_t[part], gp_c[...], preferred_element_type=F32)
+            proj = jnp.dot(skipx[b], w_v[:, columns], preferred_element_type=F32)
+            projx[b, 8 : 8 + ext] = proj.astype(BF16).astype(F32)
+        for b in range(batch):
+            for h in range(2):
+                grads(j, b, h)
+        for base in range(0, channels, 256):
+            part = slice(base, base + 256)
+            chunk = jnp.dot(skip_t[part], gp_v[:, columns], preferred_element_type=F32)
             own[j, part] = chunk[:, :LANES]
             core_out[j, part] = chunk[:, LANES:]
-
         core_copy(j).start()
 
         @pl.when(j > 0)
@@ -263,19 +258,12 @@
 
     scatter(STEPS - 1)
 
-    @pl.loop(0, rows // 128)
-    def _(i):
-        part = pl.ds(aligned(i * 128, 128), 128)
-        ig_v[part] = lax.dot_general(
-            gp_v[part], w_v[...], (((1,), (1,)), ((), ())), preferred_element_type=F32
-        ).astype(BF16)
-
-    stores = [
-        pltpu.make_async_copy(ig_v.at[pl.ds(b * length, length)], ig_hbm.at[b], out_sem.at[b])
-        for b in range(batch)
-    ]
-    for store in stores:
-        store.start()
+    for base in range(0, length, 128):
+        for b in range(batch):
+            ig_ref[b, base : base + 128] = lax.dot_general(
+                gp_v[b * length + base : b * length + base + 128], w_v[...],
+                (((1,), (1,)), ((), ())), preferred_element_type=F32,
+            ).astype(BF16)
 
     @pl.when(core == 0)
     def _():
@@ -317,32 +305,53 @@
         total = s2[place, i].astype(F32)
         for e in range(1, 8):
             total = total + r2[e, i].astype(F32)
-        s3[i] = total
-
-    def slot(zz):
-        return jnp.where(core == y_hi, lax.div(zz, 3), lax.div(zz, 4))
+        s3[i] = total.astype(BF16)
+
+    parity = lax.rem(core + y_hi, 2)
+
+    def tiles(zz, cc):
+        start = zz * 80 + cc * 40
+        return lax.div(start, LANES), lax.div(start + 39, LANES)
+
+    def third(e, act):
+        zz, cc = lax.rem(z + lax.div(e, 2), Z), lax.rem(core + e, 2)
+        lead, trail = tiles(zz, cc)
+        tile = jnp.where(lax.rem(lead, 2) == parity, lead, trail)
+
+        @pl.when(lax.rem(tile, 2) == parity)
+        def _():
+            act(pltpu.make_async_remote_copy(
+                src_ref=s3.at[lax.div(tile, 2)], dst_ref=r3.at[lax.rem(e, 2), lax.div(e, 2)],
+                send_sem=s3_send.at[e], recv_sem=r3_recv.at[lax.rem(e, 2)],
+                device_id=device(x, y, zz, cc), device_id_type=MESH,
+            ))
 
     @pl.loop(1, 16)
     def _(e):
-        to = lax.rem(z + lax.div(e, 2), Z)
-        pltpu.make_async_remote_copy(
-            src_ref=s3.at[slot(to)], dst_ref=r3.at[e], send_sem=s3_send, recv_sem=r3_recv,
-            device_id=device(x, y, to, lax.rem(core + e, 2)), device_id_type=MESH,
-        ).start()
-
-    pltpu.make_async_copy(r3.at[1:16], r3.at[1:16], r3_recv).wait()
-    mine, other = s3[slot(z)], r3[1]
+        third(e, lambda copy: copy.start())
+
+    lead, trail = tiles(z, core)
+    lead_mine, trail_mine = lax.rem(lead, 2) == parity, lax.rem(trail, 2) == parity
+
+    @pl.when(lead_mine | trail_mine)
+    def _():
+        pltpu.make_async_copy(r3.at[0, 1:8], r3.at[0, 1:8], r3_recv.at[0]).wait()
+
+    @pl.when(jnp.logical_not(lead_mine & trail_mine))
+    def _():
+        pltpu.make_async_copy(r3.at[1], r3.at[1], r3_recv.at[1]).wait()
+
+    mine = s3[lax.div(jnp.where(lead_mine, lead, trail), 2)].astype(F32)
+    other = r3[1, 0].astype(F32)
     for e in range(1, 8):
-        mine = mine + r3[2 * e]
-        other = other + r3[2 * e + 1]
-    start = z * 80 + core * 40
-    tile, offset = lax.div(start, LANES), lax.rem(start, LANES)
-    mine_first = lax.rem(tile + core + y_hi, 2) == 0
+        mine = mine + r3[0, e].astype(F32)
+        other = other + r3[1, e].astype(F32)
+    offset = lax.rem(z * 80 + core * 40, LANES)
     mine, other = mine.reshape(24, LANES), other.reshape(24, LANES)
-    lead = jnp.where(mine_first, mine, other)
-    trail = jnp.where(mine_first, other, mine)
+    first_tile = jnp.where(lead_mine, mine, other)
+    second_tile = jnp.where(lead_mine, other, mine)
     lane = lax.broadcasted_iota(jnp.int32, (24, LANES), 1)
-    joined = jnp.where(lane >= offset, lead, trail)
+    joined = jnp.where(lane >= offset, first_tile, second_tile)
     turned = pltpu.roll(joined, lax.rem(LANES - offset, LANES), 1)
     wg_ref[...] = turned[:, :40] * (1.0 / (batch * X * Y_LO))
 
@@ -373,9 +382,10 @@
             pltpu.make_async_copy(r1y.at[0, 0:4], r1y.at[0, 0:4], s1_send.at[j]).wait()
 
     pltpu.make_async_copy(s2.at[0:7], s2.at[0:7], s2_send).wait()
-    pltpu.make_async_copy(r3.at[0:15], r3.at[0:15], s3_send).wait()
-    for store in stores:
-        store.wait()
+
+    @pl.loop(1, 16)
+    def _(e):
+        third(e, lambda copy: copy.wait_send())
 
 
 def on_device(skip_input, upstream, proj_weight, depth_kernel):
@@ -388,8 +398,8 @@
     return pl.pallas_call(
         kernel,
         out_shape=(
-            jax.ShapeDtypeStruct((batch, length, channels), BF16),
-            jax.ShapeDtypeStruct((24, 40), F32),
+            pltpu.VMEM((batch, length, channels), BF16),
+            pltpu.VMEM((24, 40), F32),
         ),
         in_specs=[
             pl.BlockSpec(memory_space=pl.ANY),
@@ -397,18 +407,18 @@
             pl.BlockSpec(memory_space=pl.ANY),
             pl.BlockSpec(memory_space=vmem),
         ],
-        out_specs=(pl.BlockSpec(memory_space=pl.ANY), pl.BlockSpec(memory_space=vmem)),
+        out_specs=(pl.BlockSpec(memory_space=vmem), pl.BlockSpec(memory_space=vmem)),
         scratch_shapes=[
             vmem((batch, ext, channels), BF16),
             vmem((batch, ext, wide), BF16),
+            vmem((batch, 2 * EDGE, wide), BF16),
             vmem((channels, wide), BF16),
             vmem((channels, rows), BF16),
-            vmem((batch, ext + 16, wide), F32),
-            vmem((ext, LANES), F32),
-            vmem((ext, LANES), F32),
-            vmem((ext, LANES), F32),
+            vmem((batch, ext + 16, 2 * LANES), F32),
+            vmem((batch, ext, 2 * LANES), F32),
+            vmem((batch, ext, 2 * LANES), F32),
+            vmem((batch, ext, 2 * LANES), F32),
             vmem((rows, wide), BF16),
-            vmem((rows, 2 * LANES), BF16),
             vmem((STEPS, channels, LANES), F32),
             vmem((STEPS, channels, LANES), F32),
             vmem((STEPS, channels, LANES), F32),
@@ -417,15 +427,15 @@
             vmem((3, Y, X, 3, 8, LANES), BF16),
             vmem((8, 3, 3, 8, LANES), BF16),
             vmem((8, 3, 3, 8, LANES), BF16),
-            vmem((3, 3, 8, LANES), F32),
-            vmem((16, 3, 8, LANES), F32),
-            vmem((rows, channels), BF16),
-            dma((3,)), dma((4,)), dma((4,)), dma((STEPS,)), dma((STEPS,)),
+            vmem((3, 3, 8, LANES), BF16),
+            vmem((2, 8, 3, 8, LANES), BF16),
+            dma, dma((STEPS, 2)), dma((STEPS, 2)),
+            dma((4,)), dma((4,)), dma((STEPS,)), dma((STEPS,)),
             dma((STEPS,)), dma((STEPS,)), dma((3,)),
-            dma, dma, dma, dma, dma((2,)),
+            dma, dma, dma((16,)), dma((2,)),
         ],
         compiler_params=pltpu.CompilerParams(
-            collective_id=0, has_side_effects=True, vmem_limit_bytes=56 * 1024 * 1024
+            collective_id=0, has_side_effects=True, vmem_limit_bytes=61 * 1024 * 1024
         ),
         cost_estimate=pl.CostEstimate(flops=3 * 10**9, bytes_accessed=5 * 10**6, transcendentals=0),
     )(skip_input, upstream, proj_weight, depth_kernel)

time: 71.2 us -> 64.1 us (0.900)
  Pallas kernels: 66.9 us -> 61.8 us
  local copies, waits for them, and re-layouts: 3.37 us -> 1.48 us
    pallas_call x1, Pallas kernels: 66.9 us -> 61.8 us  [on_device(): pl.pallas_call(kernel, out_shape=(pltpu.VMEM((batch, length, channels), B...]
    unnamed x2, local copies, waits for them, and re-layouts: 3.37 us -> 1.48 us
where the time goes in v2:
time: 64.1 us; the launch traced here: 63.9 us
  Pallas kernels  61.8 us (96%)
  local copies, waits for them, and re-layouts  1.48 us (2%)
    pallas_call x1, Pallas kernels, on_device(): pl.pallas_call(kernel, out_shape=(pltpu.VMEM((batch, length, channels), B...  61.8 us
    unnamed x2, local copies, waits for them, and re-layouts  1.48 us

profile of v2, /device:TPU:1, one launch (start us, length us, event | category | flops | bytes accessed | tf_op | source)
XLA Modules:
  0.0 63.9 jit_solution(1290226594969624987)
XLA Ops:
  0.6 61.8 %shard_map.59 = (bf16[2,256,768]{2,1,0:T(8,128)(2,1)S(1)}, f32[24,40]{1,0:T(8,128)S(1)}) custom-call(bf16[2,256,768]{2,1,0:T(8,128)(2,1)} %skip_hbm.1, bf16[2,256,1280]{2,1,0:T(8,128)(2,1)} %up_hbm.1, bf16[768,1280]{1,0:T(8,128)(2,1)} %w_hbm.1, f32[3,1280]{1,0:T(4,128)} %taps_ref.1), custom_call_target="tpu_custom_call" | custom-call | flops 3000000000 | bytes 5000000 | tf_op jit(solution)/shard_map/pallas_call | solution.py:398
  62.5 0.9 %copy.8 = bf16[2,256,768]{2,1,0:T(8,128)(2,1)} copy(bf16[2,256,768]{2,1,0:T(8,128)(2,1)S(1)} %get-tuple-element.2) | data formatting | bytes 1572864
  63.3 0.6 copy.9

commit v3 on v2

v3 whole, which is shorter than its diff:
```python
import functools
import math

import jax
import jax.numpy as jnp
from jax import lax
from jax.experimental import pallas as pl
from jax.experimental.pallas import tpu as pltpu
from jax.sharding import PartitionSpec as P

MESH = pl.DeviceIdType.MESH
F32 = jnp.float32
BF16 = jnp.bfloat16
LANES = 128
EDGE, HALO = 16, 8
BLOCK, BLOCK2 = 64, 64
Z, Y_LO, X, Y = 8, 4, 8, 8
STEPS = 5
WAVES = ((0, 3), (3, 5))
C0 = math.sqrt(2.0 / math.pi)
CUBE = 0.044715 / (C0 * C0)


def aligned(value, by):
    return pl.multiple_of(value, by)


def kernel(
    skip_hbm, up_hbm, w_hbm, taps_ref, ig_ref, wg_ref,
    skip_v, up_v, edge_skip, edge_up, w_v, skip_t, projx, proj_next, edge_proj, a_buf, b_buf, m_buf, gp_v, gp_low, gp_high, part_sum, own, core_out, core_in,
    s1, r1, s2, r2, s3, r3,
    in_sem, w_sem, up_sem, halo_send, halo_recv, core_send, core_recv, s1_send, r1_recv,
    s2_send, r2_recv, s3_send, r3_recv,
):
    seq, dp = lax.axis_index("seq"), lax.axis_index("dp")
    n_seq = 4 * Z
    core = lax.rem(seq, 2)
    z = lax.rem(lax.div(seq, 2), Z)
    y_hi = lax.div(seq, 2 * Z)
    x, y_lo = lax.div(dp, Y_LO), lax.rem(dp, Y_LO)
    y = y_hi * Y_LO + y_lo
    batch, length, channels = skip_hbm.shape
    wide = up_hbm.shape[2]
    half = wide // 2
    rows = batch * length
    ext = length + 2 * EDGE

    def device(xx, yy, zz, cc):
        return {
            "seq": lax.div(yy, Y_LO) * (2 * Z) + zz * 2 + cc,
            "dp": xx * Y_LO + lax.rem(yy, Y_LO),
        }

    def natural(j, h):
        return pl.ds(aligned(lax.rem(core + h, 2) * half + j * LANES, LANES), LANES)

    def local(j, h):
        return pl.ds(aligned((2 * j + h) * LANES, LANES), LANES)

    load_skip = pltpu.make_async_copy(skip_hbm, skip_v, in_sem)

    def load_w(j, h):
        return pltpu.make_async_copy(w_hbm.at[:, natural(j, h)], w_v.at[:, local(j, h)], w_sem.at[j, h])

    def load_up(j, h):
        return pltpu.make_async_copy(
            up_hbm.at[:, :, natural(j, h)], up_v.at[:, :, local(j, h)], up_sem.at[j, h]
        )

    load_skip.start()

    @pl.loop(0, STEPS)
    def _(j):
        for h in range(2):
            load_w(j, h).start()
            load_up(j, h).start()

    barrier = pltpu.get_barrier_semaphore()

    def greet(target):
        pl.semaphore_signal(barrier, inc=1, device_id=target, device_id_type=MESH)

    @pl.when(seq > 0)
    def _():
        greet({"seq": seq - 1, "dp": dp})

    @pl.when(seq < n_seq - 1)
    def _():
        greet({"seq": seq + 1, "dp": dp})

    @pl.loop(1, 8)
    def _(e):
        greet(device(lax.rem(x + e, X), y, z, core))
        greet(device(x, lax.rem(y + e, Y), z, core))

    @pl.loop(1, 16)
    def _(e):
        greet(device(x, y, lax.rem(z + lax.div(e, 2), Z), lax.rem(core + e, 2)))

    has_left = jnp.where(seq > 0, 1, 0)
    has_right = jnp.where(seq < n_seq - 1, 1, 0)
    pl.semaphore_wait(barrier, 29 + has_left + has_right)

    def halo(k, source, target, rows_of, side, to):
        return pltpu.make_async_remote_copy(
            src_ref=source.at[:, rows_of], dst_ref=target.at[side],
            send_sem=halo_send.at[k], recv_sem=halo_recv.at[k],
            device_id={"seq": to, "dp": dp}, device_id_type=MESH,
        )

    first, last = pl.ds(0, HALO), pl.ds(length - HALO, HALO)

    def to_right():
        return [
            halo(0, skip_hbm, edge_skip, last, 0, seq + 1), halo(1, up_hbm, edge_up, last, 0, seq + 1)
        ]

    def to_left():
        return [
            halo(2, skip_hbm, edge_skip, first, 1, seq - 1), halo(3, up_hbm, edge_up, first, 1, seq - 1)
        ]

    @pl.when(seq < n_seq - 1)
    def _():
        for copy in to_right():
            copy.start()

    @pl.when(seq > 0)
    def _():
        for copy in to_left():
            copy.start()

    @pl.when(seq == 0)
    def _():
        edge_skip[0] = jnp.zeros((batch, HALO, channels), BF16)
        edge_up[0] = jnp.zeros((batch, HALO, wide), BF16)

    @pl.when(seq == n_seq - 1)
    def _():
        edge_skip[1] = jnp.zeros((batch, HALO, channels), BF16)
        edge_up[1] = jnp.zeros((batch, HALO, wide), BF16)

    load_skip.wait()
    for b in range(batch):
        skip_t[:, b * length : (b + 1) * length] = skip_v[b].T

    def fetched(j):
        for h in range(2):
            load_w(j, h).wait()
            load_up(j, h).wait()

    def project(j, b):
        columns = pl.ds(aligned(j * 256, 256), 256)
        proj = jnp.dot(skip_v[b], w_v[:, columns], preferred_element_type=F32)
        proj_next[b] = proj.astype(BF16)

    fetched(0)
    for b in range(batch):
        project(0, b)

    @pl.loop(1, STEPS)
    def _(j):
        fetched(j)

    @pl.when(seq > 0)
    def _():
        for copy in to_right():
            copy.wait_recv()

    @pl.when(seq < n_seq - 1)
    def _():
        for copy in to_left():
            copy.wait_recv()

    edges = jnp.concatenate(
        [edge_skip[side, b].astype(F32) for side in range(2) for b in range(batch)], axis=0
    ).astype(BF16)
    edges = jnp.dot(edges, w_v[...], preferred_element_type=F32).astype(BF16).astype(F32)
    for side in range(2):
        for b in range(batch):
            start = (side * batch + b) * HALO
            edge_proj[side, b] = edges[start : start + HALO]

    def slope(p):
        m = (CUBE * p) * (p * p)
        t = jnp.tanh(p + m)
        return (1.0 + t) * (1.0 + (1.0 - t) * (p + 3.0 * m))

    def grads(j, b, h):
        here = slice(h * LANES, (h + 1) * LANES)
        k_left, k_mid, k_right = (taps_ref[i : i + 1, natural(j, h)] for i in range(3))
        k_sum, k_dif = 0.5 * (k_left + k_right), 0.5 * (k_left - k_right)
        p_mid, p_sum, p_dif = C0 * k_mid, C0 * k_sum, C0 * k_dif
        q_mid, q_sum, q_dif = 0.25 * k_mid, 0.25 * k_sum, 0.25 * k_dif

        def rows_of(base, size, up):
            near = projx[b, base : base + size + 16, here]
            before, centre, after = near[7 : 7 + size], near[8 : 8 + size], near[9 : 9 + size]
            even = p_mid * centre + p_sum * (before + after)
            odd = p_dif * (before - after)
            fwd, rev = slope(even + odd), slope(even - odd)
            both = up * (fwd + rev)
            even, odd = q_sum * both, q_dif * (up * (fwd - rev))
            part = slice(base, base + size)
            a_buf[b, part, here] = even + odd
            b_buf[b, part, here] = even - odd
            m_buf[b, part, here] = q_mid * both

        rows_of(EDGE - HALO, HALO, edge_up[0, b, :, natural(j, h)].astype(F32))
        for base in range(0, length, BLOCK):
            rows_of(EDGE + base, BLOCK, up_v[b, base : base + BLOCK, local(j, h)].astype(F32))
        rows_of(EDGE + length, HALO, edge_up[1, b, :, natural(j, h)].astype(F32))
        for base in range(0, length, BLOCK2):
            ahead = a_buf[b, base + 16 : base + 24 + BLOCK2, here][1 : 1 + BLOCK2]
            behind = b_buf[b, base + 8 : base + 16 + BLOCK2, here][7 : 7 + BLOCK2]
            value = (ahead + behind + m_buf[b, base + EDGE : base + EDGE + BLOCK2, here]).astype(BF16)
            (gp_low, gp_high)[b][base : base + BLOCK2, here] = value

    def core_copy(j):
        return pltpu.make_async_remote_copy(
            src_ref=core_out.at[j], dst_ref=core_in.at[j],
            send_sem=core_send.at[j], recv_sem=core_recv.at[j],
            device_id=device(x, y, z, 1 - core), device_id_type=MESH,
        )

    def farthest(i):
        return jnp.where(lax.rem(i, 2) == 1, 4 + lax.div(i, 2), 4 - lax.div(i, 2))

    def along_x(j, e):
        to = lax.rem(x + e, X)
        return pltpu.make_async_remote_copy(
            src_ref=s1.at[j, lax.rem(to, 2), lax.div(to, 2)], dst_ref=r1.at[j, e],
            send_sem=s1_send.at[j], recv_sem=r1_recv.at[j],
            device_id=device(to, y, z, core), device_id_type=MESH,
        )

    def along_y(j, e):
        to = lax.rem(y + e, Y)
        lines = lax.rem(1 + lax.div(to, Y_LO) + to, 2)
        return pltpu.make_async_remote_copy(
            src_ref=s1.at[j, lines, :, lax.rem(to, Y_LO)], dst_ref=r1.at[j, e],
            send_sem=s1_send.at[j], recv_sem=r1_recv.at[j],
            device_id=device(x, to, z, core), device_id_type=MESH,
        )

    def scatter(j):
        core_copy(j).wait_recv()
        for i in range(X):
            part = slice(i * 96, (i + 1) * 96)
            total = own[j, part] + core_in[j, part]
            s1[j, i % 2, i // 2] = total.reshape(Y_LO, 3, 8, LANES).astype(BF16)

        @pl.when(core == 0)
        def _():
            @pl.loop(1, 8)
            def _(i):
                along_x(j, farthest(i)).start()

            r1[j, 0] = s1[j, lax.rem(x, 2), lax.div(x, 2)]

        @pl.when(core == 1)
        def _():
            @pl.loop(1, 8)
            def _(i):
                along_y(j, farthest(i)).start()

            r1[j, 0] = s1[j, lax.rem(1 + y_hi + y_lo, 2), :, y_lo]

    def gathered(j):
        pltpu.make_async_copy(r1.at[j, 1:8], r1.at[j, 1:8], r1_recv.at[j]).wait()
        total = r1[j, 0].astype(F32)
        for e in range(1, 8):
            total = total + r1[j, e].astype(F32)
        s2[:, j] = total.astype(BF16)

    active = lax.rem(x + y_hi + y_lo + core, 2) == 0

    def second(wave, i):
        lo, hi = WAVES[wave]
        to_y = lax.rem(x + i, 2) * Y_LO + i
        to_x = 2 * i + lax.rem(1 + y_hi + y_lo, 2)
        e = jnp.where(core == 0, lax.rem(to_y + Y - y, Y), lax.rem(to_x + X - x, X))
        target = device(jnp.where(core == 0, x, to_x), jnp.where(core == 0, to_y, y), z, core)
        return e, pltpu.make_async_remote_copy(
            src_ref=s2.at[i, lo:hi], dst_ref=r2.at[e, lo:hi],
            send_sem=s2_send.at[wave, i], recv_sem=r2_recv.at[wave],
            device_id=target, device_id_type=MESH,
        )

    def send_second(wave):
        lo, hi = WAVES[wave]

        @pl.loop(0, 4)
        def _(i):
            e, copy = second(wave, i)

            @pl.when(e > 0)
            def _():
                copy.start()

            @pl.when(e == 0)
            def _():
                r2[0, lo:hi] = s2[i, lo:hi]

    def input_grad(b):
        for base in range(0, length, 128):
            ig_ref[b, base : base + 128] = lax.dot_general(
                gp_v[b * length + base : b * length + base + 128], w_v[...],
                (((1,), (1,)), ((), ())), preferred_element_type=F32,
            ).astype(BF16)

    @pl.loop(0, STEPS)
    def _(j):
        columns = pl.ds(aligned(j * 256, 256), 256)
        for b in range(batch):
            projx[b, 8 + EDGE - HALO : 8 + EDGE] = edge_proj[0, b, :, columns]
            projx[b, 8 + EDGE : 8 + EDGE + length] = proj_next[b].astype(F32)
            projx[b, 8 + EDGE + length : 8 + EDGE + length + HALO] = edge_proj[1, b, :, columns]
        for b in range(batch):
            project(lax.rem(j + 1, STEPS), b)
            for h in range(2):
                grads(j, b, h)
            piece = (gp_low, gp_high)[b][...]
            gp_v[b * length : (b + 1) * length, columns] = piece
            if b == 0:
                for base in range(0, channels, 192):
                    part_sum[base : base + 192] = jnp.dot(
                        skip_t[base : base + 192, :length], piece, preferred_element_type=F32
                    )
        for base in range(0, channels, 192):
            chunk = part_sum[base : base + 192] + jnp.dot(
                skip_t[base : base + 192, length:], gp_high[...], preferred_element_type=F32
            )
            for i in range(0, 192, 24):
                row = (base + i) // 24
                flip = (row // Y_LO + row) % 2
                part = slice(base + i, base + i + 24)
                own[j, part] = chunk[i : i + 24, flip * LANES : (flip + 1) * LANES]
                core_out[j, part] = chunk[i : i + 24, (1 - flip) * LANES : (2 - flip) * LANES]
        core_copy(j).start()

        @pl.when(j > 0)
        def _():
            scatter(j - 1)

    input_grad(0)
    scatter(STEPS - 1)
    for j in range(*WAVES[0]):
        gathered(j)
    send_second(0)
    input_grad(1)
    for j in range(*WAVES[1]):
        gathered(j)
    send_second(1)

    def tiles(zz, cc):
        start = zz * 80 + cc * 40
        return lax.div(start, LANES), lax.div(start + 39, LANES)

    def third(e, act):
        zz, cc = lax.rem(z + lax.div(e, 2), Z), lax.rem(core + e, 2)
        lead, trail = tiles(zz, cc)

        def copy(k, tile):
            return pltpu.make_async_remote_copy(
                src_ref=s3.at[tile], dst_ref=r3.at[k, lax.div(e, 2)],
                send_sem=s3_send.at[k, e], recv_sem=r3_recv.at[k],
                device_id=device(x, y, zz, cc), device_id_type=MESH,
            )

        act(copy(0, lead))

        @pl.when(trail > lead)
        def _():
            act(copy(1, trail))

    my_lead, my_trail = tiles(z, core)

    @pl.when(active)
    def _():
        for wave, (lo, hi) in enumerate(WAVES):
            pltpu.make_async_copy(r2.at[1:8, lo:hi], r2.at[1:8, lo:hi], r2_recv.at[wave]).wait()
            for j in range(lo, hi):
                total = r2[0, j].astype(F32)
                for e in range(1, 8):
                    total = total + r2[e, j].astype(F32)
                s3[j] = total.astype(BF16)

        @pl.loop(1, 8)
        def _(i):
            for k in range(2):
                third(2 * farthest(i) + k, lambda copy: copy.start())

        third(1, lambda copy: copy.start())
        r3[0, 0] = s3[my_lead]
        r3[1, 0] = s3[my_trail]
        pltpu.make_async_copy(r3.at[0, 1:8], r3.at[0, 1:8], r3_recv.at[0]).wait()

        @pl.when(my_trail > my_lead)
        def _():
            pltpu.make_async_copy(r3.at[1, 1:8], r3.at[1, 1:8], r3_recv.at[1]).wait()

    @pl.when(jnp.logical_not(active))
    def _():
        pltpu.make_async_copy(r3.at[0], r3.at[0], r3_recv.at[0]).wait()

        @pl.when(my_trail > my_lead)
        def _():
            pltpu.make_async_copy(r3.at[1], r3.at[1], r3_recv.at[1]).wait()

    lead, trail = r3[0, 0].astype(F32), r3[1, 0].astype(F32)
    for e in range(1, 8):
        lead = lead + r3[0, e].astype(F32)
        trail = trail + r3[1, e].astype(F32)
    lead, trail = lead.reshape(24, LANES), trail.reshape(24, LANES)
    offset = lax.rem(z * 80 + core * 40, LANES)
    lane = lax.broadcasted_iota(jnp.int32, (24, LANES), 1)
    turned = pltpu.roll(jnp.where(lane >= offset, lead, trail), lax.rem(LANES - offset, LANES), 1)
    wg_ref[...] = turned[:, :40] * (1.0 / (batch * X * Y_LO))

    @pl.when(seq < n_seq - 1)
    def _():
        for copy in to_right():
            copy.wait_send()

    @pl.when(seq > 0)
    def _():
        for copy in to_left():
            copy.wait_send()

    @pl.loop(0, STEPS)
    def _(j):
        core_copy(j).wait_send()

        pltpu.make_async_copy(r1.at[j, 0:7], r1.at[j, 0:7], s1_send.at[j]).wait()

    for wave in range(len(WAVES)):
        @pl.loop(0, 4)
        def _(i):
            e, copy = second(wave, i)

            @pl.when(e > 0)
            def _():
                copy.wait_send()

    @pl.when(active)
    def _():
        @pl.loop(1, 16)
        def _(e):
            third(e, lambda copy: copy.wait_send())


def on_device(skip_input, upstream, proj_weight, depth_kernel):
    batch, length, channels = skip_input.shape
    wide = upstream.shape[2]
    ext = length + 2 * EDGE
    rows = batch * length
    vmem = pltpu.VMEM
    dma = pltpu.SemaphoreType.DMA
    return pl.pallas_call(
        kernel,
        out_shape=(
            pltpu.VMEM((batch, length, channels), BF16),
            pltpu.VMEM((24, 40), F32),
        ),
        in_specs=[
            pl.BlockSpec(memory_space=pl.ANY),
            pl.BlockSpec(memory_space=pl.ANY),
            pl.BlockSpec(memory_space=pl.ANY),
            pl.BlockSpec(memory_space=vmem),
        ],
        out_specs=(pl.BlockSpec(memory_space=vmem), pl.BlockSpec(memory_space=vmem)),
        scratch_shapes=[
            vmem((batch, length, channels), BF16),
            vmem((batch, length, wide), BF16),
            vmem((2, batch, HALO, channels), BF16),
            vmem((2, batch, HALO, wide), BF16),
            vmem((channels, wide), BF16),
            vmem((channels, rows), BF16),
            vmem((batch, ext + 16, 2 * LANES), F32),
            vmem((batch, length, 2 * LANES), BF16),
            vmem((2, batch, HALO, wide), F32),
            vmem((batch, ext, 2 * LANES), F32),
            vmem((batch, ext, 2 * LANES), F32),
            vmem((batch, ext, 2 * LANES), F32),
            vmem((rows, wide), BF16),
            vmem((length, 2 * LANES), BF16),
            vmem((length, 2 * LANES), BF16),
            vmem((channels, 2 * LANES), F32),
            vmem((STEPS, channels, LANES), F32),
            vmem((STEPS, channels, LANES), F32),
            vmem((STEPS, channels, LANES), F32),
            vmem((STEPS, 2, 4, Y_LO, 3, 8, LANES), BF16),
            vmem((STEPS, 8, 4, 3, 8, LANES), BF16),
            vmem((4, STEPS, 3, 8, LANES), BF16),
            vmem((8, STEPS, 3, 8, LANES), BF16),
            vmem((STEPS, 3, 8, LANES), BF16),
            vmem((2, 8, 3, 8, LANES), BF16),
            dma, dma((STEPS, 2)), dma((STEPS, 2)),
            dma((4,)), dma((4,)), dma((STEPS,)), dma((STEPS,)),
            dma((STEPS,)), dma((STEPS,)),
            dma((2, 4)), dma((2,)), dma((2, 16)), dma((2,)),
        ],
        compiler_params=pltpu.CompilerParams(
            collective_id=0, has_side_effects=True, vmem_limit_bytes=61 * 1024 * 1024
        ),
        cost_estimate=pl.CostEstimate(flops=3 * 10**9, bytes_accessed=5 * 10**6, transcendentals=0),
    )(skip_input, upstream, proj_weight, depth_kernel)


def solution(mesh):
    return jax.shard_map(
        on_device,
        mesh=mesh,
        in_specs=(P("dp", "seq", None), P("dp", "seq", None), P(), P()),
        out_specs=(P("dp", "seq", None), P("dp", "seq")),
        check_vma=False,
    )
```

time: 64.1 us -> 60.1 us (0.938)
  Pallas kernels: 61.8 us -> 57.8 us
    pallas_call x1, Pallas kernels: 61.8 us -> 57.8 us  [on_device(): pl.pallas_call(kernel, out_shape=(pltpu.VMEM((batch, length, channels), B...]
where the time goes in v3:
time: 60.1 us; the launch traced here: 59.9 us
  Pallas kernels  57.8 us (96%)
  local copies, waits for them, and re-layouts  1.48 us (2%)
  between operations  0.64 us (1%)
    pallas_call x1, Pallas kernels, on_device(): pl.pallas_call(kernel, out_shape=(pltpu.VMEM((batch, length, channels), B...  57.8 us
    unnamed x2, local copies, waits for them, and re-layouts  1.48 us

profile of v3, /device:TPU:1, one launch (start us, length us, event | category | flops | bytes accessed | tf_op | source)
XLA Modules:
  0.0 59.9 jit_solution(5405039322946499948)
XLA Ops:
  0.6 57.8 %shard_map.59 = (bf16[2,256,768]{2,1,0:T(8,128)(2,1)S(1)}, f32[24,40]{1,0:T(8,128)S(1)}) custom-call(bf16[2,256,768]{2,1,0:T(8,128)(2,1)} %skip_hbm.1, bf16[2,256,1280]{2,1,0:T(8,128)(2,1)} %up_hbm.1, bf16[768,1280]{1,0:T(8,128)(2,1)} %w_hbm.1, f32[3,1280]{1,0:T(4,128)} %taps_ref.1), custom_call_target="tpu_custom_call" | custom-call | flops 3000000000 | bytes 5000000 | tf_op jit(solution)/shard_map/pallas_call | solution.py:460
  58.4 0.9 %copy.8 = bf16[2,256,768]{2,1,0:T(8,128)(2,1)} copy(bf16[2,256,768]{2,1,0:T(8,128)(2,1)S(1)} %get-tuple-element.2) | data formatting | bytes 1572864
  59.3 0.6 copy.9

commit v4 on v3

--- a/solution.py
+++ b/solution.py
@@ -67,6 +67,32 @@
             up_hbm.at[:, :, natural(j, h)], up_v.at[:, :, local(j, h)], up_sem.at[j, h]
         )
 
+    barrier = pltpu.get_barrier_semaphore()
+
+    def greet(target):
+        pl.semaphore_signal(barrier, inc=1, device_id=target, device_id_type=MESH)
+
+    @pl.when(seq > 0)
+    def _():
+        greet({"seq": seq - 1, "dp": dp})
+
+    @pl.when(seq < n_seq - 1)
+    def _():
+        greet({"seq": seq + 1, "dp": dp})
+
+    def farthest(i):
+        return jnp.where(lax.rem(i, 2) == 1, 4 + lax.div(i, 2), 4 - lax.div(i, 2))
+
+    @pl.loop(1, 8)
+    def _(i):
+        e = farthest(i)
+        greet(device(lax.rem(x + e, X), y, z, core))
+        greet(device(x, lax.rem(y + e, Y), z, core))
+        for other in range(2):
+            greet(device(x, y, lax.rem(z + e, Z), lax.rem(core + other, 2)))
+
+    greet(device(x, y, z, 1 - core))
+
     load_skip.start()
 
     @pl.loop(0, STEPS)
@@ -74,28 +100,6 @@
         for h in range(2):
             load_w(j, h).start()
             load_up(j, h).start()
-
-    barrier = pltpu.get_barrier_semaphore()
-
-    def greet(target):
-        pl.semaphore_signal(barrier, inc=1, device_id=target, device_id_type=MESH)
-
-    @pl.when(seq > 0)
-    def _():
-        greet({"seq": seq - 1, "dp": dp})
-
-    @pl.when(seq < n_seq - 1)
-    def _():
-        greet({"seq": seq + 1, "dp": dp})
-
-    @pl.loop(1, 8)
-    def _(e):
-        greet(device(lax.rem(x + e, X), y, z, core))
-        greet(device(x, lax.rem(y + e, Y), z, core))
-
-    @pl.loop(1, 16)
-    def _(e):
-        greet(device(x, y, lax.rem(z + lax.div(e, 2), Z), lax.rem(core + e, 2)))
 
     has_left = jnp.where(seq > 0, 1, 0)
     has_right = jnp.where(seq < n_seq - 1, 1, 0)
@@ -222,9 +226,6 @@
             send_sem=core_send.at[j], recv_sem=core_recv.at[j],
             device_id=device(x, y, z, 1 - core), device_id_type=MESH,
         )
-
-    def farthest(i):
-        return jnp.where(lax.rem(i, 2) == 1, 4 + lax.div(i, 2), 4 - lax.div(i, 2))
 
     def along_x(j, e):
         to = lax.rem(x + e, X)
@@ -394,6 +395,38 @@
         third(1, lambda copy: copy.start())
         r3[0, 0] = s3[my_lead]
         r3[1, 0] = s3[my_trail]
+
+    @pl.when(seq < n_seq - 1)
+    def _():
+        for copy in to_right():
+            copy.wait_send()
+
+    @pl.when(seq > 0)
+    def _():
+        for copy in to_left():
+            copy.wait_send()
+
+    @pl.loop(0, STEPS)
+    def _(j):
+        core_copy(j).wait_send()
+
+        pltpu.make_async_copy(r1.at[j, 0:7], r1.at[j, 0:7], s1_send.at[j]).wait()
+
+    for wave in range(len(WAVES)):
+        @pl.loop(0, 4)
+        def _(i):
+            e, copy = second(wave, i)
+
+            @pl.when(e > 0)
+            def _():
+                copy.wait_send()
+
+    @pl.when(active)
+    def _():
+        @pl.loop(1, 16)
+        def _(e):
+            third(e, lambda copy: copy.wait_send())
+
         pltpu.make_async_copy(r3.at[0, 1:8], r3.at[0, 1:8], r3_recv.at[0]).wait()
 
         @pl.when(my_trail > my_lead)
@@ -417,37 +450,6 @@
     lane = lax.broadcasted_iota(jnp.int32, (24, LANES), 1)
     turned = pltpu.roll(jnp.where(lane >= offset, lead, trail), lax.rem(LANES - offset, LANES), 1)
     wg_ref[...] = turned[:, :40] * (1.0 / (batch * X * Y_LO))
-
-    @pl.when(seq < n_seq - 1)
-    def _():
-        for copy in to_right():
-            copy.wait_send()
-
-    @pl.when(seq > 0)
-    def _():
-        for copy in to_left():
-            copy.wait_send()
-
-    @pl.loop(0, STEPS)
-    def _(j):
-        core_copy(j).wait_send()
-
-        pltpu.make_async_copy(r1.at[j, 0:7], r1.at[j, 0:7], s1_send.at[j]).wait()
-
-    for wave in range(len(WAVES)):
-        @pl.loop(0, 4)
-        def _(i):
-            e, copy = second(wave, i)
-
-            @pl.when(e > 0)
-            def _():
-                copy.wait_send()
-
-    @pl.when(active)
-    def _():
-        @pl.loop(1, 16)
-        def _(e):
-            third(e, lambda copy: copy.wait_send())
 
 
 def on_device(skip_input, upstream, proj_weight, depth_kernel):

time: 60.1 us -> 59.2 us (0.985)
  Pallas kernels: 57.8 us -> 56.9 us
    pallas_call x1, Pallas kernels: 57.8 us -> 56.9 us  [on_device(): pl.pallas_call(kernel, out_shape=(pltpu.VMEM((batch, length, channels), B...]
where the time goes in v4:
time: 59.2 us; the launch traced here: 59 us
  Pallas kernels  56.9 us (96%)
  local copies, waits for them, and re-layouts  1.48 us (2%)
  between operations  0.64 us (1%)
    pallas_call x1, Pallas kernels, on_device(): pl.pallas_call(kernel, out_shape=(pltpu.VMEM((batch, length, channels), B...  56.9 us
    unnamed x2, local copies, waits for them, and re-layouts  1.48 us

profile of v4, /device:TPU:1, one launch (start us, length us, event | category | flops | bytes accessed | tf_op | source)
XLA Modules:
  0.0 59.0 jit_solution(11802497188773386090)
XLA Ops:
  0.6 56.9 %shard_map.59 = (bf16[2,256,768]{2,1,0:T(8,128)(2,1)S(1)}, f32[24,40]{1,0:T(8,128)S(1)}) custom-call(bf16[2,256,768]{2,1,0:T(8,128)(2,1)} %skip_hbm.1, bf16[2,256,1280]{2,1,0:T(8,128)(2,1)} %up_hbm.1, bf16[768,1280]{1,0:T(8,128)(2,1)} %w_hbm.1, f32[3,1280]{1,0:T(4,128)} %taps_ref.1), custom_call_target="tpu_custom_call" | custom-call | flops 3000000000 | bytes 5000000 | tf_op jit(solution)/shard_map/pallas_call | solution.py:462
  57.5 0.9 %copy.8 = bf16[2,256,768]{2,1,0:T(8,128)(2,1)} copy(bf16[2,256,768]{2,1,0:T(8,128)(2,1)S(1)} %get-tuple-element.2) | data formatting | bytes 1572864
  58.4 0.6 %copy.9 = f32[24,40]{1,0:T(8,128)} copy(f32[24,40]{1,0:T(8,128)S(1)} %get-tuple-element.3) | data formatting | bytes 7680

commit v5 on v4

--- a/solution.py
+++ b/solution.py
@@ -16,7 +16,7 @@
 BLOCK, BLOCK2 = 64, 64
 Z, Y_LO, X, Y = 8, 4, 8, 8
 STEPS = 5
-WAVES = ((0, 3), (3, 5))
+WAVES = ((0, 4), (4, 5))
 C0 = math.sqrt(2.0 / math.pi)
 CUBE = 0.044715 / (C0 * C0)
 
@@ -346,10 +346,10 @@
 
     input_grad(0)
     scatter(STEPS - 1)
+    input_grad(1)
     for j in range(*WAVES[0]):
         gathered(j)
     send_second(0)
-    input_grad(1)
     for j in range(*WAVES[1]):
         gathered(j)
     send_second(1)

time: 59.2 us -> 58.4 us (0.986)
  Pallas kernels: 56.9 us -> 56 us
    pallas_call x1, Pallas kernels: 56.9 us -> 56 us  [on_device(): pl.pallas_call(kernel, out_shape=(pltpu.VMEM((batch, length, channels), B...]
where the time goes in v5:
time: 58.4 us; the launch traced here: 58.2 us
  Pallas kernels  56 us (96%)
  local copies, waits for them, and re-layouts  1.48 us (3%)
  between operations  0.64 us (1%)
    pallas_call x1, Pallas kernels, on_device(): pl.pallas_call(kernel, out_shape=(pltpu.VMEM((batch, length, channels), B...  56 us
    unnamed x2, local copies, waits for them, and re-layouts  1.48 us

profile of v5, /device:TPU:1, one launch (start us, length us, event | category | flops | bytes accessed | tf_op | source)
XLA Modules:
  0.0 58.2 jit_solution(12967524006956741513)
XLA Ops:
  0.6 56.0 %shard_map.59 = (bf16[2,256,768]{2,1,0:T(8,128)(2,1)S(1)}, f32[24,40]{1,0:T(8,128)S(1)}) custom-call(bf16[2,256,768]{2,1,0:T(8,128)(2,1)} %skip_hbm.1, bf16[2,256,1280]{2,1,0:T(8,128)(2,1)} %up_hbm.1, bf16[768,1280]{1,0:T(8,128)(2,1)} %w_hbm.1, f32[3,1280]{1,0:T(4,128)} %taps_ref.1), custom_call_target="tpu_custom_call" | custom-call | flops 3000000000 | bytes 5000000 | tf_op jit(solution)/shard_map/pallas_call | solution.py:462
  56.7 0.9 %copy.8 = bf16[2,256,768]{2,1,0:T(8,128)(2,1)} copy(bf16[2,256,768]{2,1,0:T(8,128)(2,1)S(1)} %get-tuple-element.2) | data formatting | bytes 1572864
  57.6 0.6 %copy.9 = f32[24,40]{1,0:T(8,128)} copy(f32[24,40]{1,0:T(8,128)S(1)} %get-tuple-element.3) | data formatting | bytes 7680
